TPU v7x, 32 devices: a whole 2x2x4 slice. The times are simulated.
32 devices in a mesh: shard: 16 (over z, x, core), replica: 2 (over y).
Axes of the slice: x: 2, y: 2, z: 4, core: 2. Of those that a mesh axis runs over, the one named last changes fastest.
Arguments:
- tokens: float32 [4096, 1024], P(('shard', 'replica')), may hold values from -6 to 6
- segment_ids: int32 [32, 128], P(('shard', 'replica')), may hold values from 0 to 3, never falling along the last dimension, each value on 1 to 64 neighbouring positions
- cotangent: float32 [4096, 1024], P(('shard', 'replica')), may hold values from -6 to 6
- norm1_gain: bfloat16 [1024], P('shard'), may hold values from 0.099609375 to 1.8984375
- norm1_shift: bfloat16 [1024], P('shard'), may hold values from -3 to 3
- qkv_weight: bfloat16 [1024, 3072], P('shard'), may hold values from -0.1875 to 0.1875
- query_bias: bfloat16 [1024], P('shard'), may hold values from -3 to 3
- value_bias: bfloat16 [1024], P('shard'), may hold values from -3 to 3
- out_weight: bfloat16 [1024, 1024], P('shard'), may hold values from -0.75 to 0.75
- out_bias: bfloat16 [1024], P('shard'), may hold values from -3 to 3
- norm2_gain: bfloat16 [1024], P('shard'), may hold values from 0.099609375 to 1.8984375
- norm2_shift: bfloat16 [1024], P('shard'), may hold values from -3 to 3
- fc_weight: bfloat16 [1024, 4096], P('shard'), may hold values from -0.1875 to 0.1875
- fc_bias: bfloat16 [4096], P('shard'), may hold values from -3 to 3
- proj_weight: bfloat16 [4096, 1024], P('shard'), may hold values from -0.09375 to 0.09375
- proj_bias: bfloat16 [1024], P('shard'), may hold values from -3 to 3
Outputs:
- output: float32 [4096, 1024], P(('shard', 'replica'))
- tokens_grad: float32 [4096, 1024], P(('shard', 'replica'))
- norm1_gain_grad: float32 [1024], P('shard')
- norm1_shift_grad: float32 [1024], P('shard')
- qkv_weight_grad: float32 [1024, 3072], P('shard')
- query_bias_grad: float32 [1024], P('shard')
- value_bias_grad: float32 [1024], P('shard')
- out_weight_grad: float32 [1024, 1024], P('shard')
- out_bias_grad: float32 [1024], P('shard')
- norm2_gain_grad: float32 [1024], P('shard')
- norm2_shift_grad: float32 [1024], P('shard')
- fc_weight_grad: float32 [1024, 4096], P('shard')
- fc_bias_grad: float32 [4096], P('shard')
- proj_weight_grad: float32 [4096, 1024], P('shard')
- proj_bias_grad: float32 [1024], P('shard')
Inputs may be any that keep to these rules, and one draw needn't show every extreme that they name: `segment_ids`: in each row (one device's tokens) the numbers never fall, every number from 0 to 3 occurs as one run of 1 to 64 positions, and one run holds exactly 64.
All inputs are finite; a program needn't handle non-finite values.
Results may differ from a plain program's by a relative error of at most 0.012.
Values may be sent and summed in bfloat16 or wider, within the bound.
A program may use at most 192 MiB of HBM per device.

v0:
```python
import jax
import jax.numpy as jnp
from jax import lax
from jax.sharding import PartitionSpec as P

HEADS = 16
HEAD = 64
EPS = 1e-05
GELU_C = 0.7978845608028654
GELU_A = 0.044715


def layer_norm(values, gain, shift):
    row_mean = jnp.mean(values, axis=-1, keepdims=True)
    centered = values - row_mean
    inv_std = lax.rsqrt(jnp.mean(centered * centered, axis=-1, keepdims=True) + EPS)
    normed = centered * inv_std
    return (normed * gain.astype(jnp.float32) + shift.astype(jnp.float32), normed, inv_std)


def norm_back(grad_out, normed, inv_std, gain):
    scaled = grad_out * gain.astype(jnp.float32)
    return inv_std * (
        scaled
        - jnp.mean(scaled, axis=-1, keepdims=True)
        - normed * jnp.mean(scaled * normed, axis=-1, keepdims=True)
    )


def gelu_pair(pre_act):
    tangent = jnp.tanh(GELU_C * (pre_act + GELU_A * pre_act * pre_act * pre_act))
    value = 0.5 * pre_act * (1.0 + tangent)
    slope = 0.5 * (1.0 + tangent) + 0.5 * pre_act * (1.0 - tangent * tangent) * GELU_C * (
        1.0 + 3.0 * GELU_A * pre_act * pre_act
    )
    return (value, slope)


def contract(left, right, left_axis, right_axis):
    return lax.dot_general(
        left, right, (((left_axis,), (right_axis,)), ((), ())), preferred_element_type=jnp.float32
    )


def masked_scores(query, keyed, segment_row, scale):
    rows = query.shape[0]
    scores = jnp.einsum("qhd,khd->hqk", query, keyed, preferred_element_type=jnp.float32) * scale
    position = jnp.arange(rows)
    allowed = (segment_row[:, None] == segment_row[None, :]) & (
        position[None, :] <= position[:, None]
    )
    return jnp.where(allowed[None], scores, -1e30)


def on_device(
    tokens,
    segment_ids,
    cotangent,
    norm1_gain,
    norm1_shift,
    qkv_weight,
    query_bias,
    value_bias,
    out_weight,
    out_bias,
    norm2_gain,
    norm2_shift,
    fc_weight,
    fc_bias,
    proj_weight,
    proj_bias,
):
    rows, width = tokens.shape
    segment_row = segment_ids[0]
    scale = HEAD ** (-0.5)
    gain1, shift1, w_qkv, bias_query, bias_value, w_out, bias_out = (
        lax.all_gather(norm1_gain, "shard", axis=0, tiled=True),
        lax.all_gather(norm1_shift, "shard", axis=0, tiled=True),
        lax.all_gather(qkv_weight, "shard", axis=0, tiled=True),
        lax.all_gather(query_bias, "shard", axis=0, tiled=True),
        lax.all_gather(value_bias, "shard", axis=0, tiled=True),
        lax.all_gather(out_weight, "shard", axis=0, tiled=True),
        lax.all_gather(out_bias, "shard", axis=0, tiled=True),
    )
    ln1, normed1, inv1 = layer_norm(tokens, gain1, shift1)
    input1 = ln1.astype(jnp.bfloat16)
    qkv_bias = jnp.concatenate(
        [
            bias_query.astype(jnp.float32),
            jnp.zeros((width,), jnp.float32),
            bias_value.astype(jnp.float32),
        ]
    )
    projected = jnp.dot(input1, w_qkv, preferred_element_type=jnp.float32) + qkv_bias
    query = projected[:, :width].reshape(rows, HEADS, HEAD).astype(jnp.bfloat16)
    keyed = projected[:, width : 2 * width].reshape(rows, HEADS, HEAD).astype(jnp.bfloat16)
    valued = projected[:, 2 * width :].reshape(rows, HEADS, HEAD).astype(jnp.bfloat16)
    scores = masked_scores(query, keyed, segment_row, scale)
    top = jnp.max(scores, axis=-1, keepdims=True)
    log_total = top + jnp.log(jnp.sum(jnp.exp(scores - top), axis=-1, keepdims=True))
    probs_low = jnp.exp(scores - log_total).astype(jnp.bfloat16)
    context = jnp.einsum("hqk,khd->qhd", probs_low, valued, preferred_element_type=jnp.float32)
    context = context.reshape(rows, width).astype(jnp.bfloat16)
    middle = (
        tokens
        + jnp.dot(context, w_out, preferred_element_type=jnp.float32)
        + bias_out.astype(jnp.float32)
    )
    gain2, shift2, w_fc, bias_fc, w_proj, bias_proj = (
        lax.all_gather(norm2_gain, "shard", axis=0, tiled=True),
        lax.all_gather(norm2_shift, "shard", axis=0, tiled=True),
        lax.all_gather(fc_weight, "shard", axis=0, tiled=True),
        lax.all_gather(fc_bias, "shard", axis=0, tiled=True),
        lax.all_gather(proj_weight, "shard", axis=0, tiled=True),
        lax.all_gather(proj_bias, "shard", axis=0, tiled=True),
    )
    ln2, normed2, inv2 = layer_norm(middle, gain2, shift2)
    input2 = ln2.astype(jnp.bfloat16)
    pre_act = jnp.dot(input2, w_fc, preferred_element_type=jnp.float32) + bias_fc.astype(
        jnp.float32
    )
    gelu_value, gelu_slope = gelu_pair(pre_act)
    activated = gelu_value.astype(jnp.bfloat16)
    output = (
        middle
        + jnp.dot(activated, w_proj, preferred_element_type=jnp.float32)
        + bias_proj.astype(jnp.float32)
    )
    grad_proj_bias = jnp.sum(cotangent, axis=0)
    cot_low = cotangent.astype(jnp.bfloat16)
    grad_pre = contract(cot_low, w_proj, 1, 1) * gelu_slope
    grad_fc_bias = jnp.sum(grad_pre, axis=0)
    grad_pre_low = grad_pre.astype(jnp.bfloat16)
    grad_fc_weight = contract(input2, grad_pre_low, 0, 0)
    grad_in2 = contract(grad_pre_low, w_fc, 1, 1)
    grad_gain2 = jnp.sum(grad_in2 * normed2, axis=0)
    grad_shift2 = jnp.sum(grad_in2, axis=0)
    grad_middle = cotangent + norm_back(grad_in2, normed2, inv2, gain2)
    grad_proj_weight = contract(activated, cot_low, 0, 0)
    (
        share_gain2,
        share_shift2,
        share_fc_weight,
        share_fc_bias,
        share_proj_weight,
        share_proj_bias,
    ) = (
        lax.psum_scatter(grad_gain2, "shard", scatter_dimension=0, tiled=True),
        lax.psum_scatter(grad_shift2, "shard", scatter_dimension=0, tiled=True),
        lax.psum_scatter(grad_fc_weight, "shard", scatter_dimension=0, tiled=True),
        lax.psum_scatter(grad_fc_bias, "shard", scatter_dimension=0, tiled=True),
        lax.psum_scatter(grad_proj_weight, "shard", scatter_dimension=0, tiled=True),
        lax.psum_scatter(grad_proj_bias, "shard", scatter_dimension=0, tiled=True),
    )
    (
        share_gain2,
        share_shift2,
        share_fc_weight,
        share_fc_bias,
        share_proj_weight,
        share_proj_bias,
    ) = lax.psum(
        (
            share_gain2,
            share_shift2,
            share_fc_weight,
            share_fc_bias,
            share_proj_weight,
            share_proj_bias,
        ),
        "replica",
    )
    grad_out_bias = jnp.sum(grad_middle, axis=0)
    mid_low = grad_middle.astype(jnp.bfloat16)
    grad_out_weight = contract(context, mid_low, 0, 0)
    grad_context = contract(mid_low, w_out, 1, 1)
    grad_context = grad_context.reshape(rows, HEADS, HEAD).astype(jnp.bfloat16)
    again_scores = masked_scores(query, keyed, segment_row, scale)
    probs = jnp.exp(again_scores - log_total)
    probs_low = probs.astype(jnp.bfloat16)
    grad_value = jnp.einsum(
        "hqk,qhd->khd", probs_low, grad_context, preferred_element_type=jnp.float32
    )
    grad_probs = jnp.einsum(
        "qhd,khd->hqk", grad_context, valued, preferred_element_type=jnp.float32
    )
    grad_scores = probs * (grad_probs - jnp.sum(probs * grad_probs, axis=-1, keepdims=True)) * scale
    grad_scores = grad_scores.astype(jnp.bfloat16)
    grad_query = jnp.einsum("hqk,khd->qhd", grad_scores, keyed, preferred_element_type=jnp.float32)
    grad_key = jnp.einsum("hqk,qhd->khd", grad_scores, query, preferred_element_type=jnp.float32)
    grad_query = grad_query.reshape(rows, width)
    grad_key = grad_key.reshape(rows, width)
    grad_value = grad_value.reshape(rows, width)
    grad_query_bias = jnp.sum(grad_query, axis=0)
    grad_value_bias = jnp.sum(grad_value, axis=0)
    grad_qkv = jnp.concatenate([grad_query, grad_key, grad_value], axis=1).astype(jnp.bfloat16)
    grad_qkv_weight = contract(input1, grad_qkv, 0, 0)
    grad_in1 = contract(grad_qkv, w_qkv, 1, 1)
    grad_gain1 = jnp.sum(grad_in1 * normed1, axis=0)
    grad_shift1 = jnp.sum(grad_in1, axis=0)
    tokens_grad = grad_middle + norm_back(grad_in1, normed1, inv1, gain1)
    (
        share_gain1,
        share_shift1,
        share_qkv_weight,
        share_query_bias,
        share_value_bias,
        share_out_weight,
        share_out_bias,
    ) = (
        lax.psum_scatter(grad_gain1, "shard", scatter_dimension=0, tiled=True),
        lax.psum_scatter(grad_shift1, "shard", scatter_dimension=0, tiled=True),
        lax.psum_scatter(grad_qkv_weight, "shard", scatter_dimension=0, tiled=True),
        lax.psum_scatter(grad_query_bias, "shard", scatter_dimension=0, tiled=True),
        lax.psum_scatter(grad_value_bias, "shard", scatter_dimension=0, tiled=True),
        lax.psum_scatter(grad_out_weight, "shard", scatter_dimension=0, tiled=True),
        lax.psum_scatter(grad_out_bias, "shard", scatter_dimension=0, tiled=True),
    )
    (
        share_gain1,
        share_shift1,
        share_qkv_weight,
        share_query_bias,
        share_value_bias,
        share_out_weight,
        share_out_bias,
    ) = lax.psum(
        (
            share_gain1,
            share_shift1,
            share_qkv_weight,
            share_query_bias,
            share_value_bias,
            share_out_weight,
            share_out_bias,
        ),
        "replica",
    )
    return (
        output,
        tokens_grad,
        share_gain1,
        share_shift1,
        share_qkv_weight,
        share_query_bias,
        share_value_bias,
        share_out_weight,
        share_out_bias,
        share_gain2,
        share_shift2,
        share_fc_weight,
        share_fc_bias,
        share_proj_weight,
        share_proj_bias,
    )


def solution(mesh):
    in_specs = (
        P(("shard", "replica"), None),
        P(("shard", "replica"), None),
        P(("shard", "replica"), None),
        P("shard"),
        P("shard"),
        P("shard", None),
        P("shard"),
        P("shard"),
        P("shard", None),
        P("shard"),
        P("shard"),
        P("shard"),
        P("shard", None),
        P("shard"),
        P("shard", None),
        P("shard"),
    )
    out_specs = (
        P(("shard", "replica"), None),
        P(("shard", "replica"), None),
        P("shard"),
        P("shard"),
        P("shard", None),
        P("shard"),
        P("shard"),
        P("shard", None),
        P("shard"),
        P("shard"),
        P("shard"),
        P("shard", None),
        P("shard"),
        P("shard", None),
        P("shard"),
    )
    return jax.shard_map(
        on_device, mesh=mesh, in_specs=in_specs, out_specs=out_specs, check_vma=False
    )
```

profile of v0, /device:TPU:0, one launch (start us, length us, event | category | flops | bytes accessed | tf_op | source)
XLA Modules:
  0.0 957.4 jit_solution(4036300594005818929)
XLA Ops:
  7.2 0.7 all-gather.6.cloned.1.call-update
  8.0 0.7 all-gather.8.cloned.1.call-update
  8.7 0.7 all-gather.10.cloned.1.call-update
  9.5 0.5 all-gather.12.cloned.1.call-update
  10.0 1.3 fusion.50
  12.0 0.8 dynamic-update-slice.3
  12.9 0.8 dynamic-update-slice.2
  13.7 0.8 dynamic-update-slice.1
  14.6 0.8 dynamic-update-slice
  15.4 0.8 dynamic-update-slice.4
  16.2 0.8 dynamic-update-slice.7
  17.1 0.8 dynamic-update-slice.6
  17.9 0.8 dynamic-update-slice.5
  18.7 64.0 %all-reduce.20 = (bf16[1024]{0:T(1024)(128)(2,1)S(1)}, bf16[1024]{0:T(1024)(128)(2,1)S(1)}, bf16[1024]{0:T(1024)(128)(2,1)S(1)}, bf16[1024]{0:T(1024)(128)(2,1)S...) all-reduce(bf16[1024]{0:T(1024)(128)(2,1)S(1)} %dynamic-update-slic, ...), channel_id=1, replica_groups=mesh['shard'=16,'replica'=2] {'shard'}, use_global_device_ids=true, to_apply=%add.3 | all-reduce | flops 8192 | bytes 32768
  82.7 0.7 reshape.182
  83.4 17.3 %all-gather = bf16[16,1,256]{2,1,0:T(2,128)(2,1)S(1)} all-gather(bf16[1,1,256]{2,1,0:T(2,128)(2,1)S(1)} %reshape.182), channel_id=1, replica_groups=mesh['shard'=16,'replica'=2] {'shard'}, dimensions={0}, use_global_device_ids=true | all-gather | bytes 8704 | tf_op jit(solution)/shard_map/all_gather | solution.py:113
  100.8 0.1 reduce_sum.175
  100.9 0.2 multiply_reduce_fusion.6
  101.1 0.1 fusion.39
  101.3 3.8 fusion.1
  105.2 0.2 copy.51
  105.4 0.2 copy.52
  105.5 0.2 copy.53
  105.7 0.4 fusion.51
  106.1 0.2 exponential_reduce_fusion
  106.3 0.3 convolution_convert_fusion.2
  106.6 11.5 %all-gather.8.cloned.1.call-done = bf16[1024,1024]{1,0:T(8,128)(2,1)} async-done(((bf16[64,1024]{1,0:T(8,128)(2,1)}), bf16[1024,1024]{1,0:T(8,128)(2,1)}) %all-gather.8.cloned.1.call-update) | async-done | bytes 2097168 | tf_op jit(solution)/shard_map/all_gather | solution.py:82
  118.1 2.1 fusion.52
  120.2 0.2 multiply_reduce_fusion.5
  120.4 73.5 %all-gather.10.cloned.1.call-done = bf16[1024,4096]{1,0:T(8,128)(2,1)} async-done(((bf16[64,4096]{1,0:T(8,128)(2,1)}), bf16[1024,4096]{1,0:T(8,128)(2,1)}) %all-gather.10.cloned.1.call-update) | async-done | bytes 8388624 | tf_op jit(solution)/shard_map/all_gather | solution.py:112
  193.9 6.1 convolution_add_fusion
  200.0 69.1 %all-gather.12.cloned.1.call-done = bf16[4096,1024]{1,0:T(8,128)(2,1)} async-done(((bf16[256,1024]{1,0:T(8,128)(2,1)}), bf16[4096,1024]{1,0:T(8,128)(2,1)}) %all-gather.12.cloned.1.call-update) | async-done | bytes 8388624 | tf_op jit(solution)/shard_map/all_gather | solution.py:114
  269.1 7.8 fusion.55
  277.0 3.0 multiply_reduce_fusion.1
  280.0 0.3 fusion.46
  280.3 2.8 fusion.33
  283.1 0.3 reduce-scatter.5.cloned.1.call-start
  283.4 2.4 convolution_convert_fusion.1
  285.8 0.2 copy.55
  286.0 1.3 fusion.56
  287.4 2.1 convolution_convert_fusion
  289.5 2.3 fusion.49
  291.8 0.6 fusion.48
  292.3 6.8 fusion.29
  299.3 1.2 copy-done.5
  300.5 8.2 fusion.19
  308.7 1.5 copy-done.2
  310.2 9.3 fusion.36
  319.6 34.3 %reduce-scatter.7.cloned.1.call-done = f32[64,1024]{1,0:T(8,128)} async-done(((f32[1024,1024]{1,0:T(8,128)}), f32[64,1024]{1,0:T(8,128)}) %reduce-scatter.7.cloned.1.call-update) | async-done | bytes 262160 | tf_op jit(solution)/shard_map/reduce_scatter | solution.py:216
  353.9 138.2 %reduce-scatter.5.cloned.1.call-done = f32[64,3072]{1,0:T(8,128)} async-done(((f32[1024,3072]{1,0:T(8,128)}), f32[64,3072]{1,0:T(8,128)}) %reduce-scatter.5.cloned.1.call-update) | async-done | bytes 786448 | tf_op jit(solution)/shard_map/reduce_scatter | solution.py:213
  492.2 182.4 %reduce-scatter.9.cloned.1.call-done = f32[64,4096]{1,0:T(8,128)} async-done(((f32[1024,4096]{1,0:T(8,128)}), f32[64,4096]{1,0:T(8,128)}) %reduce-scatter.9.cloned.1.call-update) | async-done | bytes 1048592 | tf_op jit(solution)/shard_map/reduce_scatter | solution.py:150
  674.6 182.3 %reduce-scatter.11.cloned.1.call-done = f32[256,1024]{1,0:T(8,128)} async-done(((f32[4096,1024]{1,0:T(8,128)}), f32[256,1024]{1,0:T(8,128)}) %reduce-scatter.11.cloned.1.call-update) | async-done | bytes 1048592 | tf_op jit(solution)/shard_map/reduce_scatter | solution.py:152
  858.3 6.0 multiply_reduce_fusion.2
  864.3 59.7 %all-reduce.17 = (f32[1024]{0:T(1024)S(1)}, f32[1024]{0:T(1024)S(1)}, f32[1024]{0:T(1024)S(1)}, f32[1024]{0:T(1024)S(1)}, f32[1024]{0:T(1024)S(1)}, /*index=5*/f...) all-reduce(f32[1024]{0:T(1024)S(1)} %get-tuple-element.17, ...), channel_id=2, replica_groups=mesh['shard'=16,'replica'=2] {'shard'}, use_global_device_ids=true, to_apply=%region_12.13.clone | all-reduce | flops 12288 | bytes 98304
  924.0 0.1 dynamic-slice.9
  924.6 0.1 dynamic-slice.23
  924.7 5.7 all-reduce.18
  930.4 2.2 multiply_add_fusion.1
  932.6 5.7 fusion.13
  938.3 6.7 all-reduce.23.cloned.1.call-done
  945.0 2.2 copy.75
  947.3 1.7 copy.76
  948.9 1.0 copy.77
  949.9 1.0 copy.78
  (85 shorter events, 1.3 us)
Async XLA Ops:
  7.2 93.6 %copy-start.1 = (f32[128,1024]{1,0:T(8,128)S(1)}, f32[128,1024]{1,0:T(8,128)}, u32[]{:S(2)}) copy-start(f32[128,1024]{1,0:T(8,128)} %param.16) | copy-start | bytes 1572868
  7.2 93.9 %copy-start.17 = (s32[1,128]{1,0:T(1,128)S(1)}, s32[1,128]{1,0:T(1,128)}, u32[]{:S(2)}) copy-start(s32[1,128]{1,0:T(1,128)} %param.17) | copy-start | bytes 1540
  7.2 94.0 %all-gather.6.cloned.1.call-start = ((), (), s32[]{:S(2)}) async-start(), calls=%async_computation.4 | async-start | bytes 6684672 | tf_op jit(solution)/shard_map/all_gather | solution.py:79
  7.9 110.1 %all-gather.8.cloned.1.call-start = ((), (), s32[]{:S(2)}) async-start(), calls=%async_computation.5 | async-start | bytes 2228224 | tf_op jit(solution)/shard_map/all_gather | solution.py:82
  8.7 185.2 %all-gather.10.cloned.1.call-start = ((), (), s32[]{:S(2)}) async-start(), calls=%async_computation.6 | async-start | bytes 8912896 | tf_op jit(solution)/shard_map/all_gather | solution.py:112
  9.4 259.7 %all-gather.12.cloned.1.call-start = ((), (), s32[]{:S(2)}) async-start(), calls=%async_computation.7 | async-start | bytes 8912896 | tf_op jit(solution)/shard_map/all_gather | solution.py:114
  10.0 343.9 %reduce-scatter.7.cloned.1.call-start = ((), (), s32[]{:S(2)}) async-start(), calls=%async_computation.9 | async-start | bytes 4456448 | tf_op jit(solution)/shard_map/reduce_scatter | solution.py:216
  105.3 1.2 copy-start.6
  105.5 1.1 copy-start.11
  105.7 0.9 copy-start.9
  269.1 7.8 copy-start
  276.9 3.1 copy-start.4
  276.9 3.1 copy-start.8
  280.3 3.1 copy-start.3
  283.1 2.9 copy-start.7
  283.1 4.2 copy-start.12
  283.1 209.0 %reduce-scatter.5.cloned.1.call-start = ((), (), s32[]{:S(2)}) async-start(), calls=%async_computation.8 | async-start | bytes 13369344 | tf_op jit(solution)/shard_map/reduce_scatter | solution.py:213
  285.8 3.6 copy-start.10
  289.5 9.7 %copy-start.15 = (bf16[16,64,128]{2,1,0:T(8,128)(2,1)}, bf16[16,64,128]{2,1,0:T(8,128)(2,1)S(1)}, u32[]{:S(2)}) copy-start(bf16[16,64,128]{2,1,0:T(8,128)(2,1)S(1)} %convolution_convert_fusion) | copy-start | bytes 786436
  291.8 7.4 copy-start.16
  299.2 1.3 copy-start.5
  299.2 375.4 %reduce-scatter.9.cloned.1.call-start = ((), (), s32[]{:S(2)}) async-start(), calls=%async_computation.10 | async-start | bytes 17825792 | tf_op jit(solution)/shard_map/reduce_scatter | solution.py:150
  308.6 1.6 copy-start.2
  308.7 548.2 %reduce-scatter.11.cloned.1.call-start = ((), (), s32[]{:S(2)}) async-start(), calls=%async_computation.11 | async-start | bytes 17825792 | tf_op jit(solution)/shard_map/reduce_scatter | solution.py:152
  319.6 625.5 %all-reduce.23.cloned.1.call-start = ((), (), s32[]{:S(2)}) async-start(), calls=%async_computation.12 | async-start | bytes 6291456 | tf_op jit(solution)/shard_map/psum | solution.py:227
  945.0 3.9 copy-start.14
  945.0 4.9 copy-start.13
Sparse Core Ops, SparseCore 0:
  10.3 65.4 all-gather.5
  78.0 40.0 all-gather.7
  120.2 73.6 all-gather.9
  195.9 73.1 all-gather.11
  283.2 70.6 reduce-scatter.6
  358.4 133.7 reduce-scatter.4
  496.8 177.7 reduce-scatter.8
  679.3 177.5 reduce-scatter.10
  859.5 85.5 all-reduce.22
where the time goes:
time: 958 us; the launch traced here: 957 us
  waiting for transfers between devices  701 us (73%)
  blocking collectives  147 us (15%)
  matrix products  71 us (7%)
  local copies, waits for them, and re-layouts  18.9 us (2%)
  between operations  16.3 us (2%)
    reduce_scatter x1, waiting for transfers between devices, on_device(): lax.psum_scatter(grad_fc_weight, 'shard', scatter_dimension=0, tiled=True)  182 us
    reduce_scatter x1, waiting for transfers between devices, on_device(): lax.psum_scatter(grad_proj_weight, 'shard', scatter_dimension=0, tiled=True)  182 us
    reduce_scatter x1, waiting for transfers between devices, on_device(): lax.psum_scatter(grad_qkv_weight, 'shard', scatter_dimension=0, tiled=True)  138 us
    unnamed x2, blocking collectives  124 us
    all_gather x1, waiting for transfers between devices, on_device(): lax.all_gather(fc_weight, 'shard', axis=0, tiled=True)  73.5 us
    all_gather x1, waiting for transfers between devices, on_device(): lax.all_gather(proj_weight, 'shard', axis=0, tiled=True)  69.1 us
    dot_general x8, matrix products, contract(): lax.dot_general(left, right, (((left_axis,), (right_axis,)), ((), ())), p...  46.3 us
    reduce_scatter x1, waiting for transfers between devices, on_device(): lax.psum_scatter(grad_out_weight, 'shard', scatter_dimension=0, tiled=True)  34.3 us
  transfers between devices with their start and end apart: 9, of which 8 were waited for; matrix products, arithmetic and copies ran while one was open for 7% of the time, Pallas kernels for 0%

commit v1 on v0

--- a/solution.py
+++ b/solution.py
@@ -8,6 +8,18 @@
 EPS = 1e-05
 GELU_C = 0.7978845608028654
 GELU_A = 0.044715
+
+
+def collect(x, axis, dim):
+    ways, here = (lax.axis_size(axis), lax.axis_index(axis))
+    grown, reach = (x, 1)
+    while reach < ways:
+        theirs = lax.ppermute(grown, axis, [(d, d ^ reach) for d in range(ways)])
+        mine_first = jnp.concatenate([grown, theirs], axis=dim)
+        theirs_first = jnp.concatenate([theirs, grown], axis=dim)
+        grown = jnp.where(here & reach == 0, mine_first, theirs_first)
+        reach = 2 * reach
+    return grown
 
 
 def layer_norm(values, gain, shift):
@@ -111,7 +123,7 @@
         lax.all_gather(norm2_shift, "shard", axis=0, tiled=True),
         lax.all_gather(fc_weight, "shard", axis=0, tiled=True),
         lax.all_gather(fc_bias, "shard", axis=0, tiled=True),
-        lax.all_gather(proj_weight, "shard", axis=0, tiled=True),
+        collect(proj_weight, "shard", 0),
         lax.all_gather(proj_bias, "shard", axis=0, tiled=True),
     )
     ln2, normed2, inv2 = layer_norm(middle, gain2, shift2)

time: 958 us -> 1090 us (1.14)
  blocking collectives: 147 us -> 323 us
  waiting for transfers between devices: 701 us -> 643 us
    unnamed x2, blocking collectives: 124 us -> 299 us
    ppermute x0 -> x4, waiting for transfers between devices: none -> 102 us  [collect(): theirs = lax.ppermute(grown, axis, [(d, d ^ reach) for d in range(ways)])]
    all_gather x1, waiting for transfers between devices: 73.5 us -> 0.02 us  [on_device(): lax.all_gather(fc_weight, 'shard', axis=0, tiled=True)]
    all_gather x1 -> x0, waiting for transfers between devices: 69.1 us -> none  [on_device(): lax.all_gather(proj_weight, 'shard', axis=0, tiled=True)]
    all_gather x1, waiting for transfers between devices: 11.5 us -> 0.02 us  [on_device(): lax.all_gather(out_weight, 'shard', axis=0, tiled=True)]
  transfers between devices with their start and end apart: 9 -> 12, of which waited for: 8 -> 8; matrix products, arithmetic and copies ran while one was open for 7% -> 7% of each run, Pallas kernels for 0% -> 0%
where the time goes in v1:
time: 1090 us
  waiting for transfers between devices  643 us (59%)
  blocking collectives  323 us (30%)
  matrix products  75 us (7%)
  between operations  16.7 us (2%)
  local copies, waits for them, and re-layouts  14.1 us (1%)
  other arithmetic  13.7 us (1%)
    unnamed x2, blocking collectives  299 us
    reduce_scatter x1, waiting for transfers between devices, on_device(): lax.psum_scatter(grad_proj_weight, 'shard', scatter_dimension=0, tiled=True)  182 us
    reduce_scatter x1, waiting for transfers between devices, on_device(): lax.psum_scatter(grad_fc_weight, 'shard', scatter_dimension=0, tiled=True)  182 us
    reduce_scatter x1, waiting for transfers between devices, on_device(): lax.psum_scatter(grad_qkv_weight, 'shard', scatter_dimension=0, tiled=True)  138 us
    ppermute x4, waiting for transfers between devices, collect(): theirs = lax.ppermute(grown, axis, [(d, d ^ reach) for d in range(ways)])  102 us
    dot_general x8, matrix products, contract(): lax.dot_general(left, right, (((left_axis,), (right_axis,)), ((), ())), p...  48.7 us
    reduce_scatter x1, waiting for transfers between devices, on_device(): lax.psum_scatter(grad_out_weight, 'shard', scatter_dimension=0, tiled=True)  32.4 us
  transfers between devices with their start and end apart: 12, of which 8 were waited for; matrix products, arithmetic and copies ran while one was open for 7% of the time, Pallas kernels for 0%

profile of v1, /device:TPU:0, one launch (start us, length us, event | category | flops | bytes accessed | tf_op | source)
XLA Modules:
  0.0 1093.4 jit_solution(9629848327593549295)
XLA Ops:
  7.2 0.7 all-gather.5.cloned.1.call-update
  8.0 0.7 all-gather.7.cloned.1.call-update
  8.7 0.7 all-gather.9.cloned.1.call-update
  9.4 0.5 collective-permute-start
  10.0 1.7 collective-permute-done
  11.7 1.6 maximum_select_fusion.9
  13.4 2.9 collective-permute-start.1
  16.3 27.8 %collective-permute-done.1 = bf16[512,1024]{1,0:T(8,128)(2,1)} collective-permute-done((bf16[512,1024]{1,0:T(8,128)(2,1)S(1)}, bf16[512,1024]{1,0:T(8,128)(2,1)}, u32[]{:S(2)}, u32[]{:S(2)}) %collective-permute-start.1) | collective-permute-done | bytes 1048608 | tf_op jit(solution)/shard_map/ppermute | solution.py:17
  44.1 4.0 maximum_select_fusion.2
  48.0 1.9 collective-permute-start.2
  50.0 72.0 %collective-permute-done.2 = bf16[1024,1024]{1,0:T(8,128)(2,1)} collective-permute-done((bf16[1024,1024]{1,0:T(8,128)(2,1)S(1)}, bf16[1024,1024]{1,0:T(8,128)(2,1)}, u32[]{:S(2)}, u32[]{:S(2)}) %collective-permute-start.2) | collective-permute-done | bytes 2097184 | tf_op jit(solution)/shard_map/ppermute | solution.py:17
  122.0 4.8 maximum_select_fusion.1
  126.8 2.4 collective-permute-start.3
  129.2 0.6 fusion.55
  130.5 0.2 dynamic-update-slice.3
  130.7 0.2 dynamic-update-slice.2
  130.9 0.2 dynamic-update-slice.1
  131.2 0.2 dynamic-update-slice
  131.4 0.2 dynamic-update-slice.4
  131.6 0.2 dynamic-update-slice.7
  131.9 0.2 dynamic-update-slice.6
  132.1 0.2 dynamic-update-slice.5
  132.3 239.8 %all-reduce.20 = (bf16[1024]{0:T(1024)(128)(2,1)S(1)}, bf16[1024]{0:T(1024)(128)(2,1)S(1)}, bf16[1024]{0:T(1024)(128)(2,1)S(1)}, bf16[1024]{0:T(1024)(128)(2,1)S...) all-reduce(bf16[1024]{0:T(1024)(128)(2,1)S(1)} %dynamic-update-slic, ...), channel_id=1, replica_groups=mesh['shard'=16,'replica'=2] {'shard'}, use_global_device_ids=true, to_apply=%add.3 | all-reduce | flops 8192 | bytes 32768
  372.2 17.8 %all-gather = bf16[16,1,256]{2,1,0:T(2,128)(2,1)S(1)} all-gather(bf16[1,1,256]{2,1,0:T(2,128)(2,1)S(1)} %reshape.182), channel_id=1, replica_groups=mesh['shard'=16,'replica'=2] {'shard'}, dimensions={0}, use_global_device_ids=true | all-gather | bytes 8704 | tf_op jit(solution)/shard_map/all_gather | solution.py:125
  390.2 0.2 multiply_reduce_fusion.6
  390.5 3.8 fusion.2
  394.4 0.2 copy.51
  394.6 0.2 copy.52
  394.8 0.2 copy.53
  395.0 0.4 fusion.56
  395.5 0.3 convolution_convert_fusion.2
  395.8 2.1 fusion.57
  398.0 0.2 multiply_reduce_fusion.5
  398.3 4.9 convolution_add_fusion
  403.2 9.6 fusion.60
  412.9 3.0 multiply_reduce_fusion.1
  415.9 0.3 fusion.51
  416.2 2.8 fusion.36
  419.0 0.3 reduce-scatter.5.cloned.1.call-start
  419.3 3.1 convolution_convert_fusion.1
  422.4 1.1 copy.55
  423.5 1.3 fusion.61
  424.9 2.1 convolution_convert_fusion
  427.0 2.3 fusion.54
  429.3 0.6 fusion.53
  429.9 6.8 fusion.32
  436.8 1.2 copy-done.5
  438.0 8.2 fusion.22
  446.2 2.0 copy-done.2
  448.2 9.1 fusion.39
  457.5 32.4 %reduce-scatter.7.cloned.1.call-done = f32[64,1024]{1,0:T(8,128)} async-done(((f32[1024,1024]{1,0:T(8,128)}), f32[64,1024]{1,0:T(8,128)}) %reduce-scatter.7.cloned.1.call-update) | async-done | bytes 262160 | tf_op jit(solution)/shard_map/reduce_scatter | solution.py:228
  489.9 138.2 %reduce-scatter.5.cloned.1.call-done = f32[64,3072]{1,0:T(8,128)} async-done(((f32[1024,3072]{1,0:T(8,128)}), f32[64,3072]{1,0:T(8,128)}) %reduce-scatter.5.cloned.1.call-update) | async-done | bytes 786448 | tf_op jit(solution)/shard_map/reduce_scatter | solution.py:225
  628.0 182.3 %reduce-scatter.9.cloned.1.call-done = f32[64,4096]{1,0:T(8,128)} async-done(((f32[1024,4096]{1,0:T(8,128)}), f32[64,4096]{1,0:T(8,128)}) %reduce-scatter.9.cloned.1.call-update) | async-done | bytes 1048592 | tf_op jit(solution)/shard_map/reduce_scatter | solution.py:162
  810.3 182.3 %reduce-scatter.11.cloned.1.call-done = f32[256,1024]{1,0:T(8,128)} async-done(((f32[4096,1024]{1,0:T(8,128)}), f32[256,1024]{1,0:T(8,128)}) %reduce-scatter.11.cloned.1.call-update) | async-done | bytes 1048592 | tf_op jit(solution)/shard_map/reduce_scatter | solution.py:164
  994.0 6.0 multiply_reduce_fusion.2
  1000.0 59.6 %all-reduce.17 = (f32[1024]{0:T(1024)S(1)}, f32[1024]{0:T(1024)S(1)}, f32[1024]{0:T(1024)S(1)}, f32[1024]{0:T(1024)S(1)}, f32[1024]{0:T(1024)S(1)}, /*index=5*/f...) all-reduce(f32[1024]{0:T(1024)S(1)} %get-tuple-element.17, ...), channel_id=2, replica_groups=mesh['shard'=16,'replica'=2] {'shard'}, use_global_device_ids=true, to_apply=%region_12.13.clone | all-reduce | flops 12288 | bytes 98304
  1060.4 5.7 all-reduce.18
  1066.1 2.2 multiply_add_fusion.1
  1068.3 8.5 fusion.16
  1076.7 4.0 all-reduce.23.cloned.1.call-done
  1080.7 2.2 copy.75
  1082.9 1.7 copy.76
  1084.6 1.0 copy.77
  1085.6 1.0 copy.78
  (112 shorter events, 1.9 us)
Async XLA Ops:
  7.2 383.3 %all-gather.5.cloned.1.call-start = ((), (), s32[]{:S(2)}) async-start(), calls=%async_computation.4 | async-start | bytes 6684672 | tf_op jit(solution)/shard_map/all_gather | solution.py:91
  7.9 387.9 %all-gather.7.cloned.1.call-start = ((), (), s32[]{:S(2)}) async-start(), calls=%async_computation.5 | async-start | bytes 2228224 | tf_op jit(solution)/shard_map/all_gather | solution.py:94
  8.7 389.6 %all-gather.9.cloned.1.call-start = ((), (), s32[]{:S(2)}) async-start(), calls=%async_computation.6 | async-start | bytes 8912896 | tf_op jit(solution)/shard_map/all_gather | solution.py:124
  9.4 480.5 %reduce-scatter.7.cloned.1.call-start = ((), (), s32[]{:S(2)}) async-start(), calls=%async_computation.8 | async-start | bytes 4456448 | tf_op jit(solution)/shard_map/reduce_scatter | solution.py:228
  9.4 2.3 collective-permute-start
  13.3 2.9 copy-start.6
  13.4 30.7 %collective-permute-start.1 = (bf16[512,1024]{1,0:T(8,128)(2,1)S(1)}, bf16[512,1024]{1,0:T(8,128)(2,1)}, u32[]{:S(2)}, u32[]{:S(2)}) collective-permute-start(bf16[512,1024]{1,0:T(8,128)(2,1)S(1)} %maximum_select_fusion.9), channel_id=1, source_target_pairs={{0,4},{2,6},{4,0},{6,2},{8,12},{10,14},{12,8},{14,10},{16,20},{18,... | collective-permute-start | bytes 3145736 | tf_op jit(solution)/shard_map/ppermute | solution.py:17
  48.0 74.0 %collective-permute-start.2 = (bf16[1024,1024]{1,0:T(8,128)(2,1)S(1)}, bf16[1024,1024]{1,0:T(8,128)(2,1)}, u32[]{:S(2)}, u32[]{:S(2)}) collective-permute-start(bf16[1024,1024]{1,0:T(8,128)(2,1)S(1)} %maximum_select_fusion.2), channel_id=1, source_target_pairs={{0,8},{2,10},{4,12},{6,14},{8,0},{10,2},{12,4},{14,6},{16,24},{18,... | collective-permute-start | bytes 6291464 | tf_op jit(solution)/shard_map/ppermute | solution.py:17
  49.9 79.3 %copy-start.15 = (u32[32]{0:T(128)S(1)}, u32[32]{0:T(128)}, u32[]{:S(2)}) copy-start(u32[32]{0:T(128)} %constant.50) | copy-start | bytes 388
  49.9 80.6 %copy-start.16 = (bf16[64]{0:T(256)(128)(2,1)S(1)}, bf16[64]{0:T(256)(128)(2,1)}, u32[]{:S(2)}) copy-start(bf16[64]{0:T(256)(128)(2,1)} %param.23) | copy-start | bytes 388
  49.9 80.8 %copy-start.17 = (bf16[64]{0:T(256)(128)(2,1)S(1)}, bf16[64]{0:T(256)(128)(2,1)}, u32[]{:S(2)}) copy-start(bf16[64]{0:T(256)(128)(2,1)} %param.22) | copy-start | bytes 388
  49.9 81.0 %copy-start.18 = (bf16[64]{0:T(256)(128)(2,1)S(1)}, bf16[64]{0:T(256)(128)(2,1)}, u32[]{:S(2)}) copy-start(bf16[64]{0:T(256)(128)(2,1)} %param.20) | copy-start | bytes 388
  49.9 81.3 %copy-start.19 = (bf16[64]{0:T(256)(128)(2,1)S(1)}, bf16[64]{0:T(256)(128)(2,1)}, u32[]{:S(2)}) copy-start(bf16[64]{0:T(256)(128)(2,1)} %param.19) | copy-start | bytes 388
  49.9 81.5 %copy-start.20 = (bf16[64]{0:T(256)(128)(2,1)S(1)}, bf16[64]{0:T(256)(128)(2,1)}, u32[]{:S(2)}) copy-start(bf16[64]{0:T(256)(128)(2,1)} %param.25) | copy-start | bytes 388
  49.9 81.7 %copy-start.21 = (bf16[64]{0:T(256)(128)(2,1)S(1)}, bf16[64]{0:T(256)(128)(2,1)}, u32[]{:S(2)}) copy-start(bf16[64]{0:T(256)(128)(2,1)} %param.31) | copy-start | bytes 388
  49.9 81.9 %copy-start.22 = (bf16[64]{0:T(256)(128)(2,1)S(1)}, bf16[64]{0:T(256)(128)(2,1)}, u32[]{:S(2)}) copy-start(bf16[64]{0:T(256)(128)(2,1)} %param.27) | copy-start | bytes 388
  49.9 82.2 %copy-start.23 = (bf16[64]{0:T(256)(128)(2,1)S(1)}, bf16[64]{0:T(256)(128)(2,1)}, u32[]{:S(2)}) copy-start(bf16[64]{0:T(256)(128)(2,1)} %param.26) | copy-start | bytes 388
  50.0 322.2 %copy-start.24 = (bf16[256]{0:T(256)(128)(2,1)S(1)}, bf16[256]{0:T(256)(128)(2,1)}, u32[]{:S(2)}) copy-start(bf16[256]{0:T(256)(128)(2,1)} %param.29) | copy-start | bytes 1540
  50.0 340.0 %copy-start = (f32[128,1024]{1,0:T(8,128)S(1)}, f32[128,1024]{1,0:T(8,128)}, u32[]{:S(2)}) copy-start(f32[128,1024]{1,0:T(8,128)} %param.16) | copy-start | bytes 1572868
  50.0 340.4 %copy-start.14 = (s32[1,128]{1,0:T(1,128)S(1)}, s32[1,128]{1,0:T(1,128)}, u32[]{:S(2)}) copy-start(s32[1,128]{1,0:T(1,128)} %param.17) | copy-start | bytes 1540
  126.8 276.4 %collective-permute-start.3 = (bf16[2048,1024]{1,0:T(8,128)(2,1)}, bf16[2048,1024]{1,0:T(8,128)(2,1)}, u32[]{:S(2)}, u32[]{:S(2)}) collective-permute-start(bf16[2048,1024]{1,0:T(8,128)(2,1)} %maximum_select_fusion.1), channel_id=1, source_target_pairs={{0,16},{2,18},{4,20},{6,22},{8,24},{10,26},{12,28},{14,30},{16,0},... | collective-permute-start | bytes 12582920 | tf_op jit(solution)/shard_map/ppermute | solution.py:17
  394.8 1.0 copy-start.8
  398.2 4.9 copy-start.7
  398.2 14.6 %slice-start = ((s8[8388608]{0:T(1024)(128)(4,1)}), s8[4194304]{0:T(1024)(128)(4,1)S(1)}, s32[]{:S(2)}) async-start(s8[8388608]{0:T(1024)(128)(4,1)} %bitcast.42), calls=%async_computation.12 | async-start | bytes 8388608
  403.1 9.7 copy-start.1
  403.1 9.7 slice-start.1
  412.8 3.1 copy-start.4
  416.2 3.1 copy-start.3
  419.0 5.9 copy-start.9
  419.0 209.0 %reduce-scatter.5.cloned.1.call-start = ((), (), s32[]{:S(2)}) async-start(), calls=%async_computation.7 | async-start | bytes 13369344 | tf_op jit(solution)/shard_map/reduce_scatter | solution.py:225
  427.0 9.7 copy-start.12
  429.3 7.4 copy-start.13
  436.7 1.3 copy-start.5
  436.8 373.5 %reduce-scatter.9.cloned.1.call-start = ((), (), s32[]{:S(2)}) async-start(), calls=%async_computation.9 | async-start | bytes 17825792 | tf_op jit(solution)/shard_map/reduce_scatter | solution.py:162
  446.2 2.1 copy-start.2
  446.2 546.4 %reduce-scatter.11.cloned.1.call-start = ((), (), s32[]{:S(2)}) async-start(), calls=%async_computation.10 | async-start | bytes 17825792 | tf_op jit(solution)/shard_map/reduce_scatter | solution.py:164
  457.4 623.3 %all-reduce.23.cloned.1.call-start = ((), (), s32[]{:S(2)}) async-start(), calls=%async_computation.11 | async-start | bytes 6291456 | tf_op jit(solution)/shard_map/psum | solution.py:239
  1080.7 3.9 copy-start.11
  1080.7 4.9 copy-start.10
Sparse Core Ops, SparseCore 0:
  10.3 81.6 all-gather.4
  94.1 137.8 all-gather.6
  234.2 146.5 all-gather.8
  419.1 70.7 reduce-scatter.6
  494.3 133.6 reduce-scatter.4
  632.6 177.6 reduce-scatter.8
  815.0 177.5 reduce-scatter.10
  995.2 85.4 all-reduce.22
